TPU v7x, 32 devices: a whole 2x2x4 slice. The times are simulated.
32 devices in a mesh: shard: 4 (over z), tensor: 4 (over x, core), dp: 2 (over y).
Axes of the slice: x: 2, y: 2, z: 4, core: 2. Of those that a mesh axis runs over, the one named last changes fastest.
Arguments:
- gradient: bfloat16 [1, 8192, 8192], P(None, 'shard', ('tensor', 'dp')), may hold values from -16 to 16
- momentum: float32 [1, 8192, 8192], P(None, 'shard', ('tensor', 'dp')), may hold values from -16 to 16
- prior_right_factor: float32 [1, 8192, 128], P(None, ('tensor', 'dp')), may hold values from -8 to 8
Outputs:
- momentum_next: float32 [1, 8192, 8192], P(None, 'shard', ('tensor', 'dp'))
- following_right_factor: float32 [1, 8192, 128], P(None, ('tensor', 'dp'))
- direction: bfloat16 [1, 8192, 8192], P(None, 'shard', ('tensor', 'dp'))
All inputs are finite; a program needn't handle non-finite values.
Results may differ from a plain program's by a relative error of at most 0.0029.
Values sent between devices are 32-bit elements; how exact they have to be, the bound alone decides.
A program may use at most 64 MiB of HBM per device.

v0:
```python
import jax
import jax.numpy as jnp
from jax import lax
from jax.sharding import PartitionSpec as P

M = 8192
N = 8192
R = 128
decay_rate = 0.95
epsilon = 1e-06


def cholesky_pass(row_segment_block, summer):
    gram_matrix = summer(
        jnp.einsum(
            "ktp,ktv->kpv", row_segment_block, row_segment_block, precision=lax.Precision.HIGHEST
        )
    )
    factor_lower = jnp.linalg.cholesky(gram_matrix)
    return lax.linalg.triangular_solve(
        factor_lower, row_segment_block, left_side=False, lower=True, transpose_a=True
    )


def shards(gradient, momentum, prior_right_factor):
    mixed_update = momentum + gradient.astype(jnp.float32)
    partial_value = jnp.einsum(
        "aph,aht->apt", mixed_update, prior_right_factor, precision=lax.Precision.HIGHEST
    )
    left_full = lax.psum(partial_value, ("tensor", "dp"))

    def summer(operand):
        return lax.psum(operand, "shard")

    column_basis = cholesky_pass(cholesky_pass(left_full, summer), summer)
    right_portion = jnp.einsum(
        "wvp,wvc->wpc", mixed_update, column_basis, precision=lax.Precision.HIGHEST
    )
    fresh_right_factor = lax.psum(right_portion, "shard")
    momentum_next = mixed_update - (1.0 - decay_rate) * jnp.einsum(
        "fwd,fad->fwa", column_basis, fresh_right_factor, precision=lax.Precision.HIGHEST
    )
    squares = lax.psum(jnp.sum(fresh_right_factor * fresh_right_factor, axis=1), ("tensor", "dp"))
    scales = jnp.sqrt(squares / N + epsilon)
    following_right_factor = fresh_right_factor / scales[:, None, :]
    direction = jnp.sqrt(M / R) * jnp.einsum(
        "fwd,fad->fwa", column_basis, following_right_factor, precision=lax.Precision.HIGHEST
    )
    return (momentum_next, following_right_factor, direction.astype(jnp.bfloat16))


def solution(mesh):
    return jax.shard_map(
        shards,
        mesh=mesh,
        in_specs=(
            P(None, "shard", ("tensor", "dp")),
            P(None, "shard", ("tensor", "dp")),
            P(None, ("tensor", "dp"), None),
        ),
        out_specs=(
            P(None, "shard", ("tensor", "dp")),
            P(None, ("tensor", "dp"), None),
            P(None, "shard", ("tensor", "dp")),
        ),
        check_vma=False,
    )
```

profile of v0, /device:TPU:0, one launch (start us, length us, event | category | flops | bytes accessed | tf_op | source)
XLA Modules:
  0.0 303.4 jit_solution(12803602012103822525)
XLA Ops:
  7.2 0.0 copy-start
  7.2 0.0 all-reduce.5.cloned.1.call-start
  7.2 1.0 copy-done
  8.2 10.7 %fusion.5 = f32[1,2048,128]{2,1,0:T(8,128)} fusion(f32[1,2048,1024]{2,1,0:T(8,128)} %param.7, bf16[1,2048,1024]{2,1,0:T(8,128)(2,1)} %param.6, f32[1,1024,128]{2,1,0:T(8,128)S(1)} %copy-done), kind=kOutput, calls=%fused_computation.8 | convolution fusion | flops 3225419776 | bytes 14155776 | tf_op jit(solution)/shard_map/aph,aht->apt/dot_general | solution.py:27
  19.0 0.0 all-reduce.5.cloned.1.call-update
  19.0 0.0 all-reduce.7.cloned.1.call-start
  19.0 59.5 %all-reduce.5.cloned.1.call-done = f32[1,2048,128]{2,1,0:T(8,128)} async-done(((f32[1,2048,128]{2,1,0:T(8,128)}), f32[1,2048,128]{2,1,0:T(8,128)}) %all-reduce.5.cloned.1.call-update) | async-done | bytes 1048592 | tf_op jit(solution)/shard_map/psum | solution.py:30
  78.6 4.0 %convolution_bitcast_fusion.3 = f32[1,128,128]{1,2,0:T(8,128)} fusion(f32[1,2048,128]{2,1,0:T(8,128)} %all-reduce.5.cloned.1.call-done), kind=kOutput, calls=%fused_computation.13 | convolution fusion | flops 402653184 | bytes 1114112 | tf_op jit(solution)/shard_map/ktp,ktv->kpv/dot_general | solution.py:15
  82.5 0.0 all-reduce.7.cloned.1.call-update
  82.6 0.2 all-reduce.9.cloned.1.call-start
  82.8 33.5 %all-reduce.7.cloned.1.call-done = f32[1,128,128]{1,2,0:T(8,128)} async-done(((f32[1,128,128]{1,2,0:T(8,128)}), f32[1,128,128]{1,2,0:T(8,128)}) %all-reduce.7.cloned.1.call-update) | async-done | bytes 65552 | tf_op jit(solution)/shard_map/psum | solution.py:33
  116.3 0.9 copy.7
  117.2 0.9 fusion.21
  118.1 11.7 %custom-call.8 = f32[1,128,128]{2,1,0:T(8,128)S(1)} custom-call(f32[1,128,128]{2,1,0:T(8,128)S(1)} %fusion.21), custom_call_target="Cholesky" | custom-call | tf_op jit(solution)/shard_map/jit(cholesky)/cholesky | solution.py:19
  129.8 0.6 compare_reduce_fusion.1
  130.4 0.7 fusion.16
  131.1 9.8 %custom-call.9 = f32[1,1,128,128]{2,3,1,0:T(8,128)S(1)} custom-call(f32[1,1,128,128]{3,2,1,0:T(8,128)S(1)} %fusion.16), custom_call_target="InvertDiagBlocksLowerTriangular" | custom-call | tf_op jit(solution)/shard_map/triangular_solve/custom-call.0 | solution.py:20
  140.9 2.3 convolution_bitcast_fusion.1
  143.2 1.6 convolution_bitcast_fusion.2
  144.8 0.0 all-reduce.9.cloned.1.call-update
  144.9 0.3 all-reduce.11.cloned.1.call-start
  145.1 33.9 %all-reduce.9.cloned.1.call-done = f32[1,128,128]{1,2,0:T(8,128)} async-done(((f32[1,128,128]{1,2,0:T(8,128)}), f32[1,128,128]{1,2,0:T(8,128)}) %all-reduce.9.cloned.1.call-update) | async-done | bytes 65552 | tf_op jit(solution)/shard_map/psum | solution.py:33
  179.0 0.9 copy.9
  179.9 0.9 fusion.19
  180.8 11.7 %custom-call.10 = f32[1,128,128]{2,1,0:T(8,128)S(1)} custom-call(f32[1,128,128]{2,1,0:T(8,128)S(1)} %fusion.19), custom_call_target="Cholesky" | custom-call | tf_op jit(solution)/shard_map/jit(cholesky)/cholesky | solution.py:19
  192.5 0.6 compare_reduce_fusion
  193.2 0.7 fusion.17
  193.8 9.8 %custom-call.11 = f32[1,1,128,128]{2,3,1,0:T(8,128)S(1)} custom-call(f32[1,1,128,128]{3,2,1,0:T(8,128)S(1)} %fusion.17), custom_call_target="InvertDiagBlocksLowerTriangular" | custom-call | tf_op jit(solution)/shard_map/triangular_solve/custom-call.0 | solution.py:20
  203.7 1.1 convolution_bitcast_fusion
  204.7 17.3 %fusion.8 = f32[1,1024,128]{2,1,0:T(8,128)} fusion(f32[2048,128]{0,1:T(8,128)S(1)} %convolution_bitcast_fusion, f32[1,2048,1024]{2,1,0:T(8,128)} %param.7, bf16[1,2048,1024]{2,1,0:T(8,128)(2,1)} %param.6), kind=kOutput, calls=%fused_computation.11 | convolution fusion | flops 3225419776 | bytes 14155776 | tf_op jit(solution)/shard_map/wvp,wvc->wpc/dot_general | solution.py:36
  222.0 0.0 all-reduce.11.cloned.1.call-update
  222.0 38.4 %all-reduce.11.cloned.1.call-done = f32[1,1024,128]{2,1,0:T(8,128)} async-done(((f32[1,1024,128]{2,1,0:T(8,128)}), f32[1,1024,128]{2,1,0:T(8,128)}) %all-reduce.11.cloned.1.call-update) | async-done | bytes 524304 | tf_op jit(solution)/shard_map/psum | solution.py:39
  260.4 1.2 multiply_reduce_fusion
  261.6 13.4 %psum.39 = f32[1,128]{1,0:T(1,128)S(1)} all-reduce(f32[1,128]{1,0:T(1,128)S(1)} %bitcast.76), channel_id=1, replica_groups=mesh['shard'=4,'tensor'=4,'dp'=2] {'tensor','dp'}, use_global_device_ids=true, to_apply=%region_7.10 | all-reduce | flops 128 | bytes 1024 | tf_op jit(solution)/shard_map/psum | solution.py:43
  275.0 0.0 copy-start.1
  275.0 1.2 broadcast_divide_fusion
  276.2 0.0 copy-start.2
  276.2 8.4 %fusion.4 = bf16[1,2048,1024]{2,1,0:T(8,128)(2,1)} fusion(f32[2048,128]{0,1:T(8,128)S(1)} %convolution_bitcast_fusion, f32[1,1024,128]{2,1,0:T(8,128)S(1)} %broadcast_divide_fusion), kind=kOutput, calls=%fused_computation.7 | convolution fusion | flops 3225419776 | bytes 5767168 | tf_op jit(solution)/shard_map/fwd,fad->fwa/dot_general | solution.py:46
  284.6 0.0 copy-done.1
  284.6 12.2 %bitcast_subtract_fusion = f32[1,2048,1024]{2,1,0:T(8,128)} fusion(f32[2048,128]{0,1:T(8,128)S(1)} %convolution_bitcast_fusion, f32[1,2048,1024]{2,1,0:T(8,128)} %param.7, bf16[1,2048,1024]{2,1,0:T(8,128)(2,1)S(1)} %copy-done.1, f32[1,1024,128]{2,1,0:T(8,128)} %all-reduce.11.cloned.1.call-done), kind=kOutput, calls=%fused_computation | convolution fusion | flops 3229614080 | bytes 22544384 | tf_op jit(solution)/shard_map/fwd,fad->fwa/dot_general | solution.py:40
  296.8 0.0 copy-done.2
  (3 shorter events, 0.1 us)
Async XLA Ops:
  7.2 1.0 copy-start
  7.2 71.4 %all-reduce.5.cloned.1.call-start = ((), (), s32[]{:S(2)}) async-start(), calls=%async_computation | async-start | bytes 2097152 | tf_op jit(solution)/shard_map/psum | solution.py:30
  19.0 97.3 %all-reduce.7.cloned.1.call-start = ((), (), s32[]{:S(2)}) async-start(), calls=%async_computation.1 | async-start | bytes 131072 | tf_op jit(solution)/shard_map/psum | solution.py:33
  82.6 96.4 %all-reduce.9.cloned.1.call-start = ((), (), s32[]{:S(2)}) async-start(), calls=%async_computation.2 | async-start | bytes 131072 | tf_op jit(solution)/shard_map/psum | solution.py:33
  144.9 115.5 %all-reduce.11.cloned.1.call-start = ((), (), s32[]{:S(2)}) async-start(), calls=%async_computation.3 | async-start | bytes 1048576 | tf_op jit(solution)/shard_map/psum | solution.py:39
  275.0 9.7 %copy-start.1 = (bf16[1,2048,1024]{2,1,0:T(8,128)(2,1)S(1)}, bf16[1,2048,1024]{2,1,0:T(8,128)(2,1)}, u32[]{:S(2)}) copy-start(bf16[1,2048,1024]{2,1,0:T(8,128)(2,1)} %param.6) | copy-start | bytes 12582916
  276.2 20.6 %copy-start.2 = (f32[1,1024,128]{2,1,0:T(8,128)}, f32[1,1024,128]{2,1,0:T(8,128)S(1)}, u32[]{:S(2)}) copy-start(f32[1,1024,128]{2,1,0:T(8,128)S(1)} %broadcast_divide_fusion) | copy-start | bytes 1572868
Sparse Core Ops, SparseCore 0:
  19.1 59.4 all-reduce.4
  82.7 33.5 all-reduce.6
  145.0 33.9 all-reduce.8
  222.1 38.1 all-reduce.10
where the time goes:
time: 304 us; the launch traced here: 303 us
  waiting for transfers between devices  165 us (54%)
  matrix products  57.6 us (19%)
  other arithmetic  49.9 us (16%)
  between operations  13.9 us (5%)
  blocking collectives  13.4 us (4%)
    psum x2, waiting for transfers between devices, summer(): return lax.psum(operand, 'shard')  67.3 us
    psum x1, waiting for transfers between devices, shards(): left_full = lax.psum(partial_value, ('tensor', 'dp'))  59.5 us
    psum x1, waiting for transfers between devices, shards(): fresh_right_factor = lax.psum(right_portion, 'shard')  38.4 us
    another operation x6, other arithmetic, cholesky_pass(): factor_lower = jnp.linalg.cholesky(gram_matrix)  24.8 us
    another operation x4, other arithmetic, cholesky_pass(): lax.linalg.triangular_solve(factor_lower, row_segment_block, left_side=Fa...  20.9 us
    dot_general x1, matrix products, shards(): jnp.einsum('wvp,wvc->wpc', mixed_update, column_basis, precision=lax.Prec...  17.3 us
    psum x1, blocking collectives, shards(): lax.psum(jnp.sum(fresh_right_factor * fresh_right_factor, axis=1), ('tens...  13.4 us
    dot_general x1, matrix products, shards(): jnp.einsum('fwd,fad->fwa', column_basis, fresh_right_factor, precision=la...  12.2 us
  transfers between devices with their start and end apart: 4, of which 4 were waited for; matrix products, arithmetic and copies ran while one was open for 0% of the time, Pallas kernels for 0%

commit v1 on v0

--- a/solution.py
+++ b/solution.py
@@ -27,7 +27,8 @@
     partial_value = jnp.einsum(
         "aph,aht->apt", mixed_update, prior_right_factor, precision=lax.Precision.HIGHEST
     )
-    left_full = lax.psum(partial_value, ("tensor", "dp"))
+    all_rows = lax.psum(partial_value, "dp")
+    left_full = lax.psum(all_rows, "tensor")
 
     def summer(operand):
         return lax.psum(operand, "shard")

time: 304 us -> 327 us (1.076)
  waiting for transfers between devices: 165 us -> 189 us
    psum x1 -> x2, waiting for transfers between devices: 59.5 us -> 81.5 us  [the longest x1 42.9 us: shards(): all_rows = lax.psum(partial_value, 'dp')]
  transfers between devices with their start and end apart: 4 -> 5, of which waited for: 4 -> 5; matrix products, arithmetic and copies ran while one was open for 0% -> 0% of each run, Pallas kernels for 0% -> 0%
where the time goes in v1:
time: 327 us
  waiting for transfers between devices  189 us (58%)
  matrix products  57.6 us (18%)
  other arithmetic  49.9 us (15%)
  between operations  13.9 us (4%)
  blocking collectives  13.4 us (4%)
    psum x2, waiting for transfers between devices, summer(): return lax.psum(operand, 'shard')  68.6 us
    psum x1, waiting for transfers between devices, shards(): all_rows = lax.psum(partial_value, 'dp')  42.9 us
    psum x1, waiting for transfers between devices, shards(): left_full = lax.psum(all_rows, 'tensor')  38.6 us
    psum x1, waiting for transfers between devices, shards(): fresh_right_factor = lax.psum(right_portion, 'shard')  38.5 us
    another operation x6, other arithmetic, cholesky_pass(): factor_lower = jnp.linalg.cholesky(gram_matrix)  24.8 us
    another operation x4, other arithmetic, cholesky_pass(): lax.linalg.triangular_solve(factor_lower, row_segment_block, left_side=Fa...  20.9 us
    dot_general x1, matrix products, shards(): jnp.einsum('wvp,wvc->wpc', mixed_update, column_basis, precision=lax.Prec...  17.3 us
    psum x1, blocking collectives, shards(): lax.psum(jnp.sum(fresh_right_factor * fresh_right_factor, axis=1), ('tens...  13.4 us
  transfers between devices with their start and end apart: 5, of which 5 were waited for; matrix products, arithmetic and copies ran while one was open for 0% of the time, Pallas kernels for 0%

profile of v1, /device:TPU:0, one launch (start us, length us, event | category | flops | bytes accessed | tf_op | source)
XLA Modules:
  0.0 326.8 jit_solution(13414634869031526581)
XLA Ops:
  7.2 0.0 copy-start
  7.2 0.0 all-reduce.6.cloned.1.call-start
  7.2 1.0 copy-done
  8.2 10.7 %fusion.5 = f32[1,2048,128]{2,1,0:T(8,128)} fusion(f32[1,2048,1024]{2,1,0:T(8,128)} %param.7, bf16[1,2048,1024]{2,1,0:T(8,128)(2,1)} %param.6, f32[1,1024,128]{2,1,0:T(8,128)S(1)} %copy-done), kind=kOutput, calls=%fused_computation.8 | convolution fusion | flops 3225419776 | bytes 14155776 | tf_op jit(solution)/shard_map/aph,aht->apt/dot_general | solution.py:27
  19.0 0.0 all-reduce.6.cloned.1.call-update
  19.0 0.0 all-reduce.8.cloned.1.call-start
  19.0 42.9 %all-reduce.6.cloned.1.call-done = f32[1,2048,128]{2,1,0:T(8,128)} async-done(((f32[1,2048,128]{2,1,0:T(8,128)}), f32[1,2048,128]{2,1,0:T(8,128)}) %all-reduce.6.cloned.1.call-update) | async-done | bytes 1048592 | tf_op jit(solution)/shard_map/psum | solution.py:30
  62.0 0.0 all-reduce.8.cloned.1.call-update
  62.0 0.0 all-reduce.10.cloned.1.call-start
  62.0 38.6 %all-reduce.8.cloned.1.call-done = f32[1,2048,128]{2,1,0:T(8,128)} async-done(((f32[1,2048,128]{2,1,0:T(8,128)}), f32[1,2048,128]{2,1,0:T(8,128)}) %all-reduce.8.cloned.1.call-update) | async-done | bytes 1048592 | tf_op jit(solution)/shard_map/psum | solution.py:31
  100.6 4.0 %convolution_bitcast_fusion.3 = f32[1,128,128]{1,2,0:T(8,128)} fusion(f32[1,2048,128]{2,1,0:T(8,128)} %all-reduce.8.cloned.1.call-done), kind=kOutput, calls=%fused_computation.13 | convolution fusion | flops 402653184 | bytes 1114112 | tf_op jit(solution)/shard_map/ktp,ktv->kpv/dot_general | solution.py:15
  104.6 0.0 all-reduce.10.cloned.1.call-update
  104.7 0.2 all-reduce.12.cloned.1.call-start
  104.9 34.7 %all-reduce.10.cloned.1.call-done = f32[1,128,128]{1,2,0:T(8,128)} async-done(((f32[1,128,128]{1,2,0:T(8,128)}), f32[1,128,128]{1,2,0:T(8,128)}) %all-reduce.10.cloned.1.call-update) | async-done | bytes 65552 | tf_op jit(solution)/shard_map/psum | solution.py:34
  139.6 0.9 copy.7
  140.5 0.9 fusion.21
  141.4 11.7 %custom-call.8 = f32[1,128,128]{2,1,0:T(8,128)S(1)} custom-call(f32[1,128,128]{2,1,0:T(8,128)S(1)} %fusion.21), custom_call_target="Cholesky" | custom-call | tf_op jit(solution)/shard_map/jit(cholesky)/cholesky | solution.py:19
  153.1 0.6 compare_reduce_fusion.1
  153.8 0.7 fusion.16
  154.4 9.8 %custom-call.9 = f32[1,1,128,128]{2,3,1,0:T(8,128)S(1)} custom-call(f32[1,1,128,128]{3,2,1,0:T(8,128)S(1)} %fusion.16), custom_call_target="InvertDiagBlocksLowerTriangular" | custom-call | tf_op jit(solution)/shard_map/triangular_solve/custom-call.0 | solution.py:20
  164.2 2.3 convolution_bitcast_fusion.1
  166.5 1.6 convolution_bitcast_fusion.2
  168.1 0.0 all-reduce.12.cloned.1.call-update
  168.2 0.3 all-reduce.14.cloned.1.call-start
  168.4 33.9 %all-reduce.12.cloned.1.call-done = f32[1,128,128]{1,2,0:T(8,128)} async-done(((f32[1,128,128]{1,2,0:T(8,128)}), f32[1,128,128]{1,2,0:T(8,128)}) %all-reduce.12.cloned.1.call-update) | async-done | bytes 65552 | tf_op jit(solution)/shard_map/psum | solution.py:34
  202.3 0.9 copy.9
  203.2 0.9 fusion.19
  204.1 11.7 %custom-call.10 = f32[1,128,128]{2,1,0:T(8,128)S(1)} custom-call(f32[1,128,128]{2,1,0:T(8,128)S(1)} %fusion.19), custom_call_target="Cholesky" | custom-call | tf_op jit(solution)/shard_map/jit(cholesky)/cholesky | solution.py:19
  215.8 0.6 compare_reduce_fusion
  216.5 0.7 fusion.17
  217.2 9.8 %custom-call.11 = f32[1,1,128,128]{2,3,1,0:T(8,128)S(1)} custom-call(f32[1,1,128,128]{3,2,1,0:T(8,128)S(1)} %fusion.17), custom_call_target="InvertDiagBlocksLowerTriangular" | custom-call | tf_op jit(solution)/shard_map/triangular_solve/custom-call.0 | solution.py:20
  227.0 1.1 convolution_bitcast_fusion
  228.0 17.3 %fusion.8 = f32[1,1024,128]{2,1,0:T(8,128)} fusion(f32[2048,128]{0,1:T(8,128)S(1)} %convolution_bitcast_fusion, f32[1,2048,1024]{2,1,0:T(8,128)} %param.7, bf16[1,2048,1024]{2,1,0:T(8,128)(2,1)} %param.6), kind=kOutput, calls=%fused_computation.11 | convolution fusion | flops 3225419776 | bytes 14155776 | tf_op jit(solution)/shard_map/wvp,wvc->wpc/dot_general | solution.py:37
  245.3 0.0 all-reduce.14.cloned.1.call-update
  245.3 38.5 %all-reduce.14.cloned.1.call-done = f32[1,1024,128]{2,1,0:T(8,128)} async-done(((f32[1,1024,128]{2,1,0:T(8,128)}), f32[1,1024,128]{2,1,0:T(8,128)}) %all-reduce.14.cloned.1.call-update) | async-done | bytes 524304 | tf_op jit(solution)/shard_map/psum | solution.py:40
  283.8 1.2 multiply_reduce_fusion
  285.0 13.4 %psum.47 = f32[1,128]{1,0:T(1,128)S(1)} all-reduce(f32[1,128]{1,0:T(1,128)S(1)} %bitcast.76), channel_id=1, replica_groups=mesh['shard'=4,'tensor'=4,'dp'=2] {'tensor','dp'}, use_global_device_ids=true, to_apply=%region_8.11 | all-reduce | flops 128 | bytes 1024 | tf_op jit(solution)/shard_map/psum | solution.py:44
  298.4 0.0 copy-start.1
  298.4 1.2 broadcast_divide_fusion
  299.7 0.0 copy-start.2
  299.7 8.4 %fusion.4 = bf16[1,2048,1024]{2,1,0:T(8,128)(2,1)} fusion(f32[2048,128]{0,1:T(8,128)S(1)} %convolution_bitcast_fusion, f32[1,1024,128]{2,1,0:T(8,128)S(1)} %broadcast_divide_fusion), kind=kOutput, calls=%fused_computation.7 | convolution fusion | flops 3225419776 | bytes 5767168 | tf_op jit(solution)/shard_map/fwd,fad->fwa/dot_general | solution.py:47
  308.1 0.0 copy-done.1
  308.1 12.2 %bitcast_subtract_fusion = f32[1,2048,1024]{2,1,0:T(8,128)} fusion(f32[2048,128]{0,1:T(8,128)S(1)} %convolution_bitcast_fusion, f32[1,2048,1024]{2,1,0:T(8,128)} %param.7, bf16[1,2048,1024]{2,1,0:T(8,128)(2,1)S(1)} %copy-done.1, f32[1,1024,128]{2,1,0:T(8,128)} %all-reduce.14.cloned.1.call-done), kind=kOutput, calls=%fused_computation | convolution fusion | flops 3229614080 | bytes 22544384 | tf_op jit(solution)/shard_map/fwd,fad->fwa/dot_general | solution.py:41
  320.3 0.0 copy-done.2
  (3 shorter events, 0.1 us)
Async XLA Ops:
  7.2 1.0 copy-start
  7.2 54.8 %all-reduce.6.cloned.1.call-start = ((), (), s32[]{:S(2)}) async-start(), calls=%async_computation | async-start | bytes 2097152 | tf_op jit(solution)/shard_map/psum | solution.py:30
  19.0 81.6 %all-reduce.8.cloned.1.call-start = ((), (), s32[]{:S(2)}) async-start(), calls=%async_computation.1 | async-start | bytes 2097152 | tf_op jit(solution)/shard_map/psum | solution.py:31
  62.0 77.6 %all-reduce.10.cloned.1.call-start = ((), (), s32[]{:S(2)}) async-start(), calls=%async_computation.2 | async-start | bytes 131072 | tf_op jit(solution)/shard_map/psum | solution.py:34
  104.7 97.7 %all-reduce.12.cloned.1.call-start = ((), (), s32[]{:S(2)}) async-start(), calls=%async_computation.3 | async-start | bytes 131072 | tf_op jit(solution)/shard_map/psum | solution.py:34
  168.2 115.7 %all-reduce.14.cloned.1.call-start = ((), (), s32[]{:S(2)}) async-start(), calls=%async_computation.4 | async-start | bytes 1048576 | tf_op jit(solution)/shard_map/psum | solution.py:40
  298.4 9.7 %copy-start.1 = (bf16[1,2048,1024]{2,1,0:T(8,128)(2,1)S(1)}, bf16[1,2048,1024]{2,1,0:T(8,128)(2,1)}, u32[]{:S(2)}) copy-start(bf16[1,2048,1024]{2,1,0:T(8,128)(2,1)} %param.6) | copy-start | bytes 12582916
  299.7 20.6 %copy-start.2 = (f32[1,1024,128]{2,1,0:T(8,128)}, f32[1,1024,128]{2,1,0:T(8,128)S(1)}, u32[]{:S(2)}) copy-start(f32[1,1024,128]{2,1,0:T(8,128)S(1)} %broadcast_divide_fusion) | copy-start | bytes 1572868
Sparse Core Ops, SparseCore 0:
  19.1 42.8 all-reduce.5
  64.3 36.2 all-reduce.7
  104.8 34.7 all-reduce.9
  168.3 33.9 all-reduce.11
  245.4 38.3 all-reduce.13
